TPU v7x, 256 devices: a whole 4x4x8 slice. The times are simulated.
256 devices in a mesh: ctx: 128 (over z, x_lo, y, core), ch: 2 (over x_hi).
Axes of the slice: x: 4 (x_hi: 2, x_lo: 2; x = x_hi * 2 + x_lo), y: 4, z: 8, core: 2. Of those that a mesh axis runs over, the one named last changes fastest.
Arguments:
- query_proj: bfloat16 [32768, 2048], P('ctx', 'ch'), may hold values from -64 to 64
- key_proj: bfloat16 [32768, 2048], P('ctx', 'ch'), may hold values from -6 to 6
- value_proj: bfloat16 [32768, 2048], P('ctx', 'ch'), may hold values from -6 to 6
- filters: bfloat16 [1024, 2048], P('ctx', 'ch'), may hold values from -0.1875 to 0.1875
- cotangent: bfloat16 [32768, 2048], P('ctx', 'ch'), may hold values from -6 to 6
- stock_id: int32 [32768], P('ctx'), may hold values from 0 to 511
- stock_class: int32 [512], replicated, may hold values from 0 to 10
- cond_table: float32 [11, 2048], P(None, 'ch'), may hold values from -2.5 to 2.5
Outputs:
- normed_out: bfloat16 [32768, 2048], P('ctx', 'ch')
- grad_query: bfloat16 [32768, 2048], P('ctx', 'ch')
- grad_key: bfloat16 [32768, 2048], P('ctx', 'ch')
- grad_value: bfloat16 [32768, 2048], P('ctx', 'ch')
- grad_filter: float32 [1024, 2048], P('ctx', 'ch')
All inputs are finite; a program needn't handle non-finite values.
Results may differ from a plain program's by a relative error of at most 0.005.
Values may be sent and summed in bfloat16 or wider, within the bound.
No kernel may reach another device: no remote copies, remote signals or barrier semaphores. Data moves between devices by JAX's collectives and lax.ppermute only.
A program may use at most 128 MiB of HBM per device.

v0:
```python
import math
import jax
import jax.numpy as jnp
from jax import lax
from jax.sharding import PartitionSpec as P

REACH = 4
EPSILON = 1e-05
PRECISE = lax.Precision.HIGHEST
TRANSFORM = lax.Precision.HIGH


def from_behind(block, axis, distance):
    devices = range(lax.axis_size(axis))
    route = [(i - distance, i) for i in devices if i - distance in devices]
    return lax.ppermute(block, axis, route)


def product_tables(length, flipped):
    frequency = lax.broadcasted_iota(jnp.int32, (length, length), 0)
    position = lax.broadcasted_iota(jnp.int32, (length, length), 1)
    if flipped:
        position = length - 1 - position
    phase_index = (2 * frequency + 1) * position % (4 * length)
    angles = phase_index.astype(jnp.float32) * (math.pi / (2 * length))
    return (jnp.cos(angles), jnp.sin(angles))


def output_tables(length, flipped):
    position = lax.broadcasted_iota(jnp.int32, (length, length), 0)
    frequency = lax.broadcasted_iota(jnp.int32, (length, length), 1)
    if flipped:
        position = 2 * length - 1 - position
    else:
        position = length + position
    phase_index = (2 * frequency + 1) * position % (4 * length)
    angles = phase_index.astype(jnp.float32) * (math.pi / (2 * length))
    return (jnp.cos(angles) / length, jnp.sin(angles) / length)


def spectra(tables, pieces):
    cosine, sine_table = tables
    real_part = jnp.einsum("fs,nsc->fnc", cosine, pieces, precision=TRANSFORM)
    imag_part = -jnp.einsum("fs,nsc->fnc", sine_table, pieces, precision=TRANSFORM)
    return (real_part, imag_part)


def signals(tables, spectrum):
    cosine, sine_table = tables
    return jnp.einsum("tf,fnc->ntc", cosine, spectrum[0], precision=TRANSFORM) - jnp.einsum(
        "tf,fnc->ntc", sine_table, spectrum[1], precision=TRANSFORM
    )


def adjoint_spectra(tables, pieces):
    cosine, sine_table = tables
    real_part = jnp.einsum("tf,ntc->fnc", cosine, pieces, precision=TRANSFORM)
    imag_part = -jnp.einsum("tf,ntc->fnc", sine_table, pieces, precision=TRANSFORM)
    return (real_part, imag_part)


def complex_product(left_pair, right_pair):
    return (
        left_pair[0] * right_pair[0] - left_pair[1] * right_pair[1],
        left_pair[0] * right_pair[1] + left_pair[1] * right_pair[0],
    )


def complex_add(left_pair, right_pair):
    return (left_pair[0] + right_pair[0], left_pair[1] + right_pair[1])


def alternating(length):
    return jnp.where(jnp.arange(length) % 2 == 0, 1.0, -1.0).astype(jnp.float32)[:, None, None]


def filter_segments(tables, filter_full, length, reach_blocks):
    channels = filter_full.shape[1]
    lag_spectra = spectra(tables, filter_full.reshape(reach_blocks, length, channels))
    alternate = alternating(length)
    segments = []
    for distance in range(reach_blocks + 1):
        real_part = jnp.zeros((length, 1, channels), jnp.float32)
        imag_part = jnp.zeros((length, 1, channels), jnp.float32)
        if distance >= 1:
            real_part = lag_spectra[0][:, distance - 1 : distance]
            imag_part = lag_spectra[1][:, distance - 1 : distance]
        if distance < reach_blocks:
            real_part = real_part + alternate * lag_spectra[1][:, distance : distance + 1]
            imag_part = imag_part - alternate * lag_spectra[0][:, distance : distance + 1]
        segments.append((real_part, imag_part))
    return segments


def segment_grad(adjoint, spectrum):
    real_part = jnp.sum(adjoint[0] * spectrum[0] + adjoint[1] * spectrum[1], axis=1, keepdims=True)
    imag_part = jnp.sum(adjoint[1] * spectrum[0] - adjoint[0] * spectrum[1], axis=1, keepdims=True)
    return (real_part, imag_part)


def filter_gradient(tables, seg_grads, length, reach_blocks):
    alternate = alternating(length)
    grad_real = []
    grad_imag = []
    for lag_block in range(reach_blocks):
        grad_real.append(seg_grads[lag_block + 1][0] - alternate * seg_grads[lag_block][1])
        grad_imag.append(seg_grads[lag_block + 1][1] + alternate * seg_grads[lag_block][0])
    grad_real = jnp.concatenate(grad_real, axis=1)
    grad_imag = jnp.concatenate(grad_imag, axis=1)
    cosine, sine_table = tables
    lag_rows = jnp.einsum("fs,fmc->msc", cosine, grad_real, precision=TRANSFORM) - jnp.einsum(
        "fs,fmc->msc", sine_table, grad_imag, precision=TRANSFORM
    )
    return lag_rows.reshape(reach_blocks * length, lag_rows.shape[2])


def shards(query_proj, key_proj, value_proj, filters, cotangent, stock_id, stock_class, cond_table):
    length = key_proj.shape[0]
    local_channels = key_proj.shape[1]
    total_channels = local_channels * lax.axis_size("ch")
    forward_tables = product_tables(length, False)
    reverse_tables = product_tables(length, True)
    out_tables = output_tables(length, False)
    back_tables = output_tables(length, True)
    stock_hits = (
        stock_id[:, None] == jnp.arange(stock_class.shape[0], dtype=jnp.int32)[None, :]
    ).astype(jnp.float32)
    class_hits = (
        stock_class[:, None] == jnp.arange(cond_table.shape[0], dtype=jnp.int32)[None, :]
    ).astype(jnp.float32)
    event_class = jnp.dot(
        stock_hits, class_hits, precision=PRECISE, preferred_element_type=jnp.float32
    )
    cond_rows = jnp.dot(
        event_class, cond_table, precision=PRECISE, preferred_element_type=jnp.float32
    )
    gate_rows = query_proj.astype(jnp.float32) * (1.0 + cond_rows)
    mixed_in = (key_proj.astype(jnp.float32) * value_proj.astype(jnp.float32)).astype(jnp.bfloat16)
    filter_full = lax.all_gather(filters, "ctx", axis=0, tiled=True).astype(jnp.float32)
    segments = filter_segments(forward_tables, filter_full, length, REACH)
    neighbours = [spectra(forward_tables, mixed_in.astype(jnp.float32)[None])]
    moving = mixed_in
    for distance in range(1, REACH + 1):
        moving = from_behind(moving, "ctx", 1)
        neighbours.append(spectra(forward_tables, moving.astype(jnp.float32)[None]))
    accumulated = complex_product(segments[0], neighbours[0])
    for distance in range(1, REACH + 1):
        accumulated = complex_add(
            accumulated, complex_product(segments[distance], neighbours[distance])
        )
    conv_out = signals(out_tables, accumulated)[0]
    scaled = gate_rows * conv_out
    squares = lax.psum(jnp.sum(scaled * scaled, axis=1), "ch")
    inv_rms = lax.rsqrt(squares / total_channels + EPSILON)[:, None]
    normed = scaled * inv_rms
    normed_out = normed.astype(jnp.bfloat16)
    upstream = cotangent.astype(jnp.float32)
    inner_sum = lax.psum(jnp.sum(upstream * normed, axis=1), "ch")
    grad_scaled = inv_rms * (upstream - normed * (inner_sum / total_channels)[:, None])
    grad_query = (grad_scaled * conv_out * (1.0 + cond_rows)).astype(jnp.bfloat16)
    grad_conv = (grad_scaled * gate_rows).astype(jnp.bfloat16)
    own_reverse = spectra(reverse_tables, grad_conv.astype(jnp.float32)[None])
    accumulated = complex_product(segments[0], own_reverse)
    moving = grad_conv
    for distance in range(1, REACH + 1):
        moving = from_behind(moving, "ctx", -1)
        later_spec = spectra(reverse_tables, moving.astype(jnp.float32)[None])
        accumulated = complex_add(accumulated, complex_product(segments[distance], later_spec))
    grad_mixed = signals(back_tables, accumulated)[0]
    adjoint = adjoint_spectra(out_tables, grad_conv.astype(jnp.float32)[None])
    seg_grads = [segment_grad(adjoint, neighbours[distance]) for distance in range(REACH + 1)]
    filter_term = filter_gradient(forward_tables, seg_grads, length, REACH)
    grad_filter = lax.psum_scatter(filter_term, "ctx", scatter_dimension=0, tiled=True)
    grad_key = (grad_mixed * value_proj.astype(jnp.float32)).astype(jnp.bfloat16)
    grad_value = (grad_mixed * key_proj.astype(jnp.float32)).astype(jnp.bfloat16)
    return (normed_out, grad_query, grad_key, grad_value, grad_filter)


def solution(mesh):
    return jax.shard_map(
        shards,
        mesh=mesh,
        in_specs=(
            P("ctx", "ch"),
            P("ctx", "ch"),
            P("ctx", "ch"),
            P("ctx", "ch"),
            P("ctx", "ch"),
            P("ctx"),
            P(),
            P(None, "ch"),
        ),
        out_specs=(P("ctx", "ch"), P("ctx", "ch"), P("ctx", "ch"), P("ctx", "ch"), P("ctx", "ch")),
        check_vma=False,
    )
```

profile of v0, /device:TPU:4, one launch (start us, length us, event | category | flops | bytes accessed | tf_op | source)
XLA Modules:
  0.0 859.0 jit_solution(3938443588100111600)
XLA Ops:
  15.6 2.7 fusion.209
  18.3 2.7 fusion.222
  21.0 3.8 collective-permute-start.1
  24.7 2.7 fusion.207
  27.4 2.7 fusion.219
  30.1 2.8 collective-permute-start.2
  36.9 6.6 collective-permute-start.3
  45.6 2.7 fusion.215
  48.2 2.7 fusion.201
  53.5 172.6 %all-gather.2.cloned.1.call-done = bf16[1024,1024]{1,0:T(8,128)(2,1)} async-done(((bf16[8,1024]{1,0:T(8,128)(2,1)}), bf16[1024,1024]{1,0:T(8,128)(2,1)}) %all-gather.2.cloned.1.call-update) | async-done | bytes 2097168 | tf_op jit(solution)/shard_map/all_gather | solution.py:139
  226.1 4.0 convolution_negate_fusion
  236.0 3.8 fusion.35
  239.9 4.9 multiply_reduce_fusion
  244.8 6.4 psum.14
  252.9 6.5 psum.15
  259.4 3.7 multiply_convert_fusion
  270.0 3.8 fusion
  273.9 6.1 fusion.16
  286.1 8.4 collective-permute-done.5
  301.7 3.6 collective-permute-done.6
  312.8 3.1 collective-permute-done.7
  318.9 3.3 fusion.32
  322.2 3.6 fusion.26
  327.9 524.0 %reduce-scatter.2.cloned.1.call-done = f32[8,1024]{1,0:T(8,128)} async-done(((f32[1024,1024]{1,0:T(8,128)}), f32[8,1024]{1,0:T(8,128)}) %reduce-scatter.2.cloned.1.call-update) | async-done | bytes 32784 | tf_op jit(solution)/shard_map/reduce_scatter | solution.py:173
  (106 shorter events, 57.1 us)
Async XLA Ops:
  7.2 6.5 copy-start
  7.2 219.0 %all-gather.2.cloned.1.call-start = ((), (), s32[]{:S(2)}) async-start(), calls=%async_computation.1 | async-start | bytes 2113536 | tf_op jit(solution)/shard_map/all_gather | solution.py:139
  7.9 844.0 %reduce-scatter.2.cloned.1.call-start = ((), (), s32[]{:S(2)}) async-start(), calls=%async_computation.2 | async-start | bytes 4227072 | tf_op jit(solution)/shard_map/reduce_scatter | solution.py:173
  9.2 18.2 %copy-start.22 = (bf16[256,1024]{0,1:T(8,128)(2,1)}, bf16[256,1024]{0,1:T(8,128)(2,1)S(1)}, u32[]{:S(2)}) copy-start(bf16[256,1024]{0,1:T(8,128)(2,1)S(1)} %copy.14) | copy-start | bytes 1572868
  10.7 19.4 %copy-start.24 = (bf16[256,1024]{0,1:T(8,128)(2,1)}, bf16[256,1024]{0,1:T(8,128)(2,1)S(1)}, u32[]{:S(2)}) copy-start(bf16[256,1024]{0,1:T(8,128)(2,1)S(1)} %copy.15) | copy-start | bytes 1572868
  10.8 10.2 %collective-permute-start = (bf16[256,1024]{0,1:T(8,128)(2,1)S(1)}, bf16[256,1024]{0,1:T(8,128)(2,1)S(1)}, u32[]{:S(2)}, u32[]{:S(2)}) collective-permute-start(bf16[256,1024]{0,1:T(8,128)(2,1)S(1)} %fusion.27), channel_id=1, source_target_pairs={{0,2},{2,4},{4,6},{6,8},{8,10},{10,12},{12,14},{14,16},{16,18},{18... | collective-permute-start | bytes 1572872 | tf_op jit(solution)/shard_map/ppermute | solution.py:16
  21.0 9.1 %collective-permute-start.1 = (bf16[256,1024]{0,1:T(8,128)(2,1)S(1)}, bf16[256,1024]{0,1:T(8,128)(2,1)S(1)}, u32[]{:S(2)}, u32[]{:S(2)}) collective-permute-start(bf16[256,1024]{0,1:T(8,128)(2,1)S(1)} %collective-permute-done), channel_id=1, source_target_pairs={{0,2},{2,4},{4,6},{6,8},{8,10},{10,12},{12,14},{14,16},{16,18},{18... | collective-permute-start | bytes 1572872 | tf_op jit(solution)/shard_map/ppermute | solution.py:16
  30.1 6.8 collective-permute-start.2
  36.9 11.4 %collective-permute-start.3 = (bf16[256,1024]{0,1:T(8,128)(2,1)S(1)}, bf16[256,1024]{0,1:T(8,128)(2,1)S(1)}, u32[]{:S(2)}, u32[]{:S(2)}) collective-permute-start(bf16[256,1024]{0,1:T(8,128)(2,1)S(1)} %collective-permute-done.2), channel_id=1, source_target_pairs={{0,2},{2,4},{4,6},{6,8},{8,10},{10,12},{12,14},{14,16},{16,18},{18... | collective-permute-start | bytes 1572872 | tf_op jit(solution)/shard_map/ppermute | solution.py:16
  226.1 6.5 copy-start.18
  230.2 9.6 %copy-start.8 = (f32[256,4,1024]{2,0,1:T(8,128)}, f32[256,4,1024]{2,0,1:T(8,128)S(1)}, u32[]{:S(2)}) copy-start(f32[256,4,1024]{2,0,1:T(8,128)S(1)} %convolution_negate_fusion) | copy-start | bytes 12582916
  230.3 5.5 copy-start.14
  230.3 5.8 copy-start.16
  232.6 7.3 copy-start.10
  259.4 6.6 copy-start.3
  259.4 6.6 copy-start.5
  259.4 6.6 copy-start.7
  281.0 3.8 collective-permute-start.4
  284.8 9.7 %collective-permute-start.5 = (bf16[256,1024]{1,0:T(8,128)(2,1)S(1)}, bf16[256,1024]{1,0:T(8,128)(2,1)S(1)}, u32[]{:S(2)}, u32[]{:S(2)}) collective-permute-start(bf16[256,1024]{1,0:T(8,128)(2,1)S(1)} %collective-permute-done.4), channel_id=1, source_target_pairs={{2,0},{4,2},{6,4},{8,6},{10,8},{12,10},{14,12},{16,14},{18,16},{20... | collective-permute-start | bytes 1572872 | tf_op jit(solution)/shard_map/ppermute | solution.py:16
  294.5 10.8 %collective-permute-start.6 = (bf16[256,1024]{1,0:T(8,128)(2,1)S(1)}, bf16[256,1024]{1,0:T(8,128)(2,1)S(1)}, u32[]{:S(2)}, u32[]{:S(2)}) collective-permute-start(bf16[256,1024]{1,0:T(8,128)(2,1)S(1)} %collective-permute-done.5), channel_id=1, source_target_pairs={{2,0},{4,2},{6,4},{8,6},{10,8},{12,10},{14,12},{16,14},{18,16},{20... | collective-permute-start | bytes 1572872 | tf_op jit(solution)/shard_map/ppermute | solution.py:16
  305.3 10.6 %collective-permute-start.7 = (bf16[256,1024]{1,0:T(8,128)(2,1)S(1)}, bf16[256,1024]{1,0:T(8,128)(2,1)S(1)}, u32[]{:S(2)}, u32[]{:S(2)}) collective-permute-start(bf16[256,1024]{1,0:T(8,128)(2,1)S(1)} %collective-permute-done.6), channel_id=1, source_target_pairs={{2,0},{4,2},{6,4},{8,6},{10,8},{12,10},{14,12},{16,14},{18,16},{20... | collective-permute-start | bytes 1572872 | tf_op jit(solution)/shard_map/ppermute | solution.py:16
  308.3 10.6 %copy-start.9 = (f32[256,4,1024]{2,0,1:T(8,128)S(1)}, f32[256,4,1024]{2,0,1:T(8,128)}, u32[]{:S(2)}) copy-start(f32[256,4,1024]{2,0,1:T(8,128)} %copy-done.8) | copy-start | bytes 12582916
  308.3 10.6 %copy-start.11 = (f32[256,4,1024]{2,0,1:T(8,128)S(1)}, f32[256,4,1024]{2,0,1:T(8,128)}, u32[]{:S(2)}) copy-start(f32[256,4,1024]{2,0,1:T(8,128)} %copy-done.10) | copy-start | bytes 12582916
  322.2 529.7 %copy-start.1 = (f32[11,1024]{1,0:T(8,128)S(1)}, f32[11,1024]{1,0:T(8,128)}, u32[]{:S(2)}) copy-start(f32[11,1024]{1,0:T(8,128)} %param.15) | copy-start | bytes 135172
  (15 other events, 43.8 us)
Sparse Core Ops, SparseCore 0:
  9.9 216.2 all-gather.1
  280.1 571.7 reduce-scatter.1
where the time goes:
time: 868 us; the launch traced here: 859 us
  waiting for transfers between devices  715 us (82%)
  matrix products  77.2 us (9%)
  starting transfers between devices  20.3 us (2%)
  between operations  14.9 us (2%)
  blocking collectives  12.9 us (1%)
  local copies, waits for them, and re-layouts  10.2 us (1%)
    reduce_scatter x1, waiting for transfers between devices, shards(): lax.psum_scatter(filter_term, 'ctx', scatter_dimension=0, tiled=True)  524 us
    all_gather x1, waiting for transfers between devices, shards(): lax.all_gather(filters, 'ctx', axis=0, tiled=True).astype(jnp.float32)  173 us
    dot_general x11, matrix products, spectra(): jnp.einsum('fs,nsc->fnc', sine_table, pieces, precision=TRANSFORM)  23.5 us
    dot_general x11, matrix products, spectra(): real_part = jnp.einsum('fs,nsc->fnc', cosine, pieces, precision=TRANSFORM)  22.3 us
    ppermute x8, starting transfers between devices, from_behind(): return lax.ppermute(block, axis, route)  20.3 us
    ppermute x8, waiting for transfers between devices, from_behind(): return lax.ppermute(block, axis, route)  17.5 us
  transfers between devices with their start and end apart: 10, of which 6 were waited for; matrix products, arithmetic and copies ran while one was open for 6% of the time, Pallas kernels for 0%

commit v1 on v0

--- a/solution.py
+++ b/solution.py
@@ -136,7 +136,9 @@
     )
     gate_rows = query_proj.astype(jnp.float32) * (1.0 + cond_rows)
     mixed_in = (key_proj.astype(jnp.float32) * value_proj.astype(jnp.float32)).astype(jnp.bfloat16)
-    filter_full = lax.all_gather(filters, "ctx", axis=0, tiled=True).astype(jnp.float32)
+    filter_full = jnp.concatenate(
+        lax.all_to_all(jnp.stack([filters for _ in range(lax.axis_size("ctx"))]), "ctx", 0, 0), 0
+    ).astype(jnp.float32)
     segments = filter_segments(forward_tables, filter_full, length, REACH)
     neighbours = [spectra(forward_tables, mixed_in.astype(jnp.float32)[None])]
     moving = mixed_in

time: 868 us -> 764 us (0.88)
  waiting for transfers between devices: 715 us -> 584 us
  starting transfers between devices: 20.3 us -> 47.9 us
    all_gather x1 -> x0, waiting for transfers between devices: 173 us -> none  [shards(): lax.all_gather(filters, 'ctx', axis=0, tiled=True).astype(jnp.float32)]
    reduce_scatter x1, waiting for transfers between devices: 524 us -> 562 us  [shards(): lax.psum_scatter(filter_term, 'ctx', scatter_dimension=0, tiled=True)]
    all_to_all x0 -> x1, starting transfers between devices: none -> 14.6 us  [shards(): lax.all_to_all(jnp.stack([filters for _ in range(lax.axis_size('ctx'))]),...]
    ppermute x8, starting transfers between devices: 20.3 us -> 33.3 us  [from_behind(): return lax.ppermute(block, axis, route)]
  transfers between devices with their start and end apart: 10 -> 10, of which waited for: 6 -> 5; matrix products, arithmetic and copies ran while one was open for 6% -> 7% of each run, Pallas kernels for 0% -> 0%
where the time goes in v1:
time: 764 us; the launch traced here: 755 us
  waiting for transfers between devices  584 us (76%)
  matrix products  79.4 us (10%)
  starting transfers between devices  47.9 us (6%)
  between operations  15 us (2%)
  blocking collectives  12.9 us (2%)
  other arithmetic  8.64 us (1%)
    reduce_scatter x1, waiting for transfers between devices, shards(): lax.psum_scatter(filter_term, 'ctx', scatter_dimension=0, tiled=True)  562 us
    ppermute x8, starting transfers between devices, from_behind(): return lax.ppermute(block, axis, route)  33.3 us
    dot_general x11, matrix products, spectra(): real_part = jnp.einsum('fs,nsc->fnc', cosine, pieces, precision=TRANSFORM)  25.4 us
    dot_general x11, matrix products, spectra(): jnp.einsum('fs,nsc->fnc', sine_table, pieces, precision=TRANSFORM)  23.3 us
    ppermute x8, waiting for transfers between devices, from_behind(): return lax.ppermute(block, axis, route)  22.7 us
  transfers between devices with their start and end apart: 10, of which 5 were waited for; matrix products, arithmetic and copies ran while one was open for 7% of the time, Pallas kernels for 0%

profile of v1, /device:TPU:4, one launch (start us, length us, event | category | flops | bytes accessed | tf_op | source)
XLA Modules:
  0.0 755.2 jit_solution(4797553325605524892)
XLA Ops:
  9.6 14.6 %all-to-all-start = ((bf16[128,8,1024]{2,1,0:T(8,128)(2,1)}), bf16[128,8,1024]{2,1,0:T(8,128)(2,1)}, u32[]{:S(2)}, u32[]{:S(2)}) async-start(bf16[128,8,1024]{2,1,0:T(8,128)(2,1)} %stack.2), calls=%async_computation | async-start | bytes 4194304 | tf_op jit(solution)/shard_map/all_to_all | solution.py:140
  28.7 2.7 fusion.209
  34.1 5.6 collective-permute-start.1
  39.7 2.7 fusion.207
  42.4 2.7 fusion.219
  45.1 10.5 %collective-permute-start.2 = (bf16[256,1024]{0,1:T(8,128)(2,1)S(1)}, bf16[256,1024]{0,1:T(8,128)(2,1)S(1)}, u32[]{:S(2)}, u32[]{:S(2)}) collective-permute-start(bf16[256,1024]{0,1:T(8,128)(2,1)S(1)} %collective-permute-done.1), channel_id=1, source_target_pairs={{0,2},{2,4},{4,6},{6,8},{8,10},{10,12},{12,14},{14,16},{16,18},{18... | collective-permute-start | bytes 1572872 | tf_op jit(solution)/shard_map/ppermute | solution.py:16
  59.5 10.3 %collective-permute-start.3 = (bf16[256,1024]{0,1:T(8,128)(2,1)S(1)}, bf16[256,1024]{0,1:T(8,128)(2,1)S(1)}, u32[]{:S(2)}, u32[]{:S(2)}) collective-permute-start(bf16[256,1024]{0,1:T(8,128)(2,1)S(1)} %collective-permute-done.2), channel_id=1, source_target_pairs={{0,2},{2,4},{4,6},{6,8},{8,10},{10,12},{12,14},{14,16},{16,18},{18... | collective-permute-start | bytes 1572872 | tf_op jit(solution)/shard_map/ppermute | solution.py:16
  71.8 2.7 fusion.215
  79.8 4.0 convolution_negate_fusion
  83.8 5.4 fusion.172
  89.4 3.8 fusion.35
  93.2 4.9 multiply_reduce_fusion
  98.1 6.4 psum.14
  106.2 6.5 psum.15
  112.7 3.7 multiply_convert_fusion
  123.4 3.8 fusion
  127.2 6.1 fusion.16
  135.6 4.3 collective-permute-done.4
  141.2 12.2 %collective-permute-done.5 = bf16[256,1024]{1,0:T(8,128)(2,1)S(1)} collective-permute-done((bf16[256,1024]{1,0:T(8,128)(2,1)S(1)}, bf16[256,1024]{1,0:T(8,128)(2,1)S(1)}, u32[]{:S(2)}, u32[]{:S(2)}) %collective-permute-start.5) | collective-permute-done | bytes 524320 | tf_op jit(solution)/shard_map/ppermute | solution.py:16
  160.7 3.2 collective-permute-done.6
  171.4 3.0 collective-permute-done.7
  177.4 3.3 fusion.32
  180.7 3.6 fusion.26
  186.4 561.7 %reduce-scatter.2.cloned.1.call-done = f32[8,1024]{1,0:T(8,128)} async-done(((f32[1024,1024]{1,0:T(8,128)}), f32[8,1024]{1,0:T(8,128)}) %reduce-scatter.2.cloned.1.call-update) | async-done | bytes 32784 | tf_op jit(solution)/shard_map/reduce_scatter | solution.py:175
  (112 shorter events, 52.5 us)
Async XLA Ops:
  7.2 19.6 %copy-start = (f32[11,1024]{1,0:T(8,128)S(1)}, f32[11,1024]{1,0:T(8,128)}, u32[]{:S(2)}) copy-start(f32[11,1024]{1,0:T(8,128)} %param.15) | copy-start | bytes 135172
  7.2 17.1 %copy-start.28 = (bf16[256,1024]{1,0:T(8,128)(2,1)S(1)}, bf16[256,1024]{1,0:T(8,128)(2,1)}, u32[]{:S(2)}) copy-start(bf16[256,1024]{1,0:T(8,128)(2,1)} %param.9) | copy-start | bytes 1572868
  7.2 17.3 %copy-start.29 = (bf16[256,1024]{1,0:T(8,128)(2,1)S(1)}, bf16[256,1024]{1,0:T(8,128)(2,1)}, u32[]{:S(2)}) copy-start(bf16[256,1024]{1,0:T(8,128)(2,1)} %param.10) | copy-start | bytes 1572868
  9.6 16.8 %copy-start.30 = (s32[512]{0:T(512)S(1)}, s32[512]{0:T(512)}, u32[]{:S(2)}) copy-start(s32[512]{0:T(512)} %param.14) | copy-start | bytes 6148
  9.6 16.8 %copy-start.31 = (s32[256]{0:T(256)S(1)}, s32[256]{0:T(256)}, u32[]{:S(2)}) copy-start(s32[256]{0:T(256)} %param.13) | copy-start | bytes 3076
  9.6 70.1 %all-to-all-start = ((bf16[128,8,1024]{2,1,0:T(8,128)(2,1)}), bf16[128,8,1024]{2,1,0:T(8,128)(2,1)}, u32[]{:S(2)}, u32[]{:S(2)}) async-start(bf16[128,8,1024]{2,1,0:T(8,128)(2,1)} %stack.2), calls=%async_computation | async-start | bytes 4194304 | tf_op jit(solution)/shard_map/all_to_all | solution.py:140
  24.2 723.8 %reduce-scatter.2.cloned.1.call-start = ((), (), s32[]{:S(2)}) async-start(), calls=%async_computation.2 | async-start | bytes 4227072 | tf_op jit(solution)/shard_map/reduce_scatter | solution.py:175
  24.5 17.9 %copy-start.21 = (bf16[256,1024]{0,1:T(8,128)(2,1)}, bf16[256,1024]{0,1:T(8,128)(2,1)S(1)}, u32[]{:S(2)}) copy-start(bf16[256,1024]{0,1:T(8,128)(2,1)S(1)} %copy.14) | copy-start | bytes 1572868
  24.7 20.3 %copy-start.23 = (bf16[256,1024]{0,1:T(8,128)(2,1)}, bf16[256,1024]{0,1:T(8,128)(2,1)S(1)}, u32[]{:S(2)}) copy-start(bf16[256,1024]{0,1:T(8,128)(2,1)S(1)} %copy.15) | copy-start | bytes 1572868
  24.9 9.2 %collective-permute-start = (bf16[256,1024]{0,1:T(8,128)(2,1)S(1)}, bf16[256,1024]{0,1:T(8,128)(2,1)S(1)}, u32[]{:S(2)}, u32[]{:S(2)}) collective-permute-start(bf16[256,1024]{0,1:T(8,128)(2,1)S(1)} %fusion.27), channel_id=1, source_target_pairs={{0,2},{2,4},{4,6},{6,8},{8,10},{10,12},{12,14},{14,16},{16,18},{18... | collective-permute-start | bytes 1572872 | tf_op jit(solution)/shard_map/ppermute | solution.py:16
  34.1 11.0 %collective-permute-start.1 = (bf16[256,1024]{0,1:T(8,128)(2,1)S(1)}, bf16[256,1024]{0,1:T(8,128)(2,1)S(1)}, u32[]{:S(2)}, u32[]{:S(2)}) collective-permute-start(bf16[256,1024]{0,1:T(8,128)(2,1)S(1)} %collective-permute-done), channel_id=1, source_target_pairs={{0,2},{2,4},{4,6},{6,8},{8,10},{10,12},{12,14},{14,16},{16,18},{18... | collective-permute-start | bytes 1572872 | tf_op jit(solution)/shard_map/ppermute | solution.py:16
  45.1 14.4 %collective-permute-start.2 = (bf16[256,1024]{0,1:T(8,128)(2,1)S(1)}, bf16[256,1024]{0,1:T(8,128)(2,1)S(1)}, u32[]{:S(2)}, u32[]{:S(2)}) collective-permute-start(bf16[256,1024]{0,1:T(8,128)(2,1)S(1)} %collective-permute-done.1), channel_id=1, source_target_pairs={{0,2},{2,4},{4,6},{6,8},{8,10},{10,12},{12,14},{14,16},{16,18},{18... | collective-permute-start | bytes 1572872 | tf_op jit(solution)/shard_map/ppermute | solution.py:16
  59.5 15.0 %collective-permute-start.3 = (bf16[256,1024]{0,1:T(8,128)(2,1)S(1)}, bf16[256,1024]{0,1:T(8,128)(2,1)S(1)}, u32[]{:S(2)}, u32[]{:S(2)}) collective-permute-start(bf16[256,1024]{0,1:T(8,128)(2,1)S(1)} %collective-permute-done.2), channel_id=1, source_target_pairs={{0,2},{2,4},{4,6},{6,8},{8,10},{10,12},{12,14},{14,16},{16,18},{18... | collective-permute-start | bytes 1572872 | tf_op jit(solution)/shard_map/ppermute | solution.py:16
  79.8 9.5 %copy-start.18 = (f32[256,1024]{1,0:T(8,128)S(1)}, f32[256,1024]{1,0:T(8,128)}, u32[]{:S(2)}) copy-start(f32[256,1024]{1,0:T(8,128)} %fusion.219) | copy-start | bytes 3145732
  83.8 9.4 %copy-start.8 = (f32[256,4,1024]{2,0,1:T(8,128)}, f32[256,4,1024]{2,0,1:T(8,128)S(1)}, u32[]{:S(2)}) copy-start(f32[256,4,1024]{2,0,1:T(8,128)S(1)} %convolution_negate_fusion) | copy-start | bytes 12582916
  112.7 6.6 copy-start.5
  112.7 6.6 copy-start.7
  134.3 5.5 collective-permute-start.4
  139.9 13.5 %collective-permute-start.5 = (bf16[256,1024]{1,0:T(8,128)(2,1)S(1)}, bf16[256,1024]{1,0:T(8,128)(2,1)S(1)}, u32[]{:S(2)}, u32[]{:S(2)}) collective-permute-start(bf16[256,1024]{1,0:T(8,128)(2,1)S(1)} %collective-permute-done.4), channel_id=1, source_target_pairs={{2,0},{4,2},{6,4},{8,6},{10,8},{12,10},{14,12},{16,14},{18,16},{20... | collective-permute-start | bytes 1572872 | tf_op jit(solution)/shard_map/ppermute | solution.py:16
  153.4 10.5 %collective-permute-start.6 = (bf16[256,1024]{1,0:T(8,128)(2,1)S(1)}, bf16[256,1024]{1,0:T(8,128)(2,1)S(1)}, u32[]{:S(2)}, u32[]{:S(2)}) collective-permute-start(bf16[256,1024]{1,0:T(8,128)(2,1)S(1)} %collective-permute-done.5), channel_id=1, source_target_pairs={{2,0},{4,2},{6,4},{8,6},{10,8},{12,10},{14,12},{16,14},{18,16},{20... | collective-permute-start | bytes 1572872 | tf_op jit(solution)/shard_map/ppermute | solution.py:16
  163.9 10.5 %collective-permute-start.7 = (bf16[256,1024]{1,0:T(8,128)(2,1)S(1)}, bf16[256,1024]{1,0:T(8,128)(2,1)S(1)}, u32[]{:S(2)}, u32[]{:S(2)}) collective-permute-start(bf16[256,1024]{1,0:T(8,128)(2,1)S(1)} %collective-permute-done.6), channel_id=1, source_target_pairs={{2,0},{4,2},{6,4},{8,6},{10,8},{12,10},{14,12},{16,14},{18,16},{20... | collective-permute-start | bytes 1572872 | tf_op jit(solution)/shard_map/ppermute | solution.py:16
  166.9 10.5 %copy-start.9 = (f32[256,4,1024]{2,0,1:T(8,128)S(1)}, f32[256,4,1024]{2,0,1:T(8,128)}, u32[]{:S(2)}) copy-start(f32[256,4,1024]{2,0,1:T(8,128)} %copy-done.8) | copy-start | bytes 12582916
  166.9 10.5 %copy-start.11 = (f32[256,4,1024]{2,0,1:T(8,128)S(1)}, f32[256,4,1024]{2,0,1:T(8,128)}, u32[]{:S(2)}) copy-start(f32[256,4,1024]{2,0,1:T(8,128)} %copy-done.10) | copy-start | bytes 12582916
  180.7 567.3 %copy-start.1 = (f32[11,1024]{1,0:T(8,128)S(1)}, f32[11,1024]{1,0:T(8,128)}, u32[]{:S(2)}) copy-start(f32[11,1024]{1,0:T(8,128)} %param.15) | copy-start | bytes 135172
  (18 other events, 67.2 us)
Sparse Core Ops, SparseCore 0:
  133.4 614.5 reduce-scatter.1
